TPU v7x, 512 devices: a whole 4x8x8 slice. The times are simulated.
512 devices in a mesh: ctx: 64 (over z, x, core), grp: 8 (over y).
Axes of the slice: x: 4, y: 8, z: 8, core: 2. Of those that a mesh axis runs over, the one named last changes fastest.
Arguments:
- query: bfloat16 [8192, 8192], P('ctx', 'grp'), may hold values from -32 to 32, as said below
- key_in: bfloat16 [8192, 8192], P('ctx', 'grp'), may hold values from -6 to 6
- value: bfloat16 [8192, 8192], P('ctx', 'grp'), may hold values from -6 to 6
- filt: bfloat16 [1024, 512], P('ctx', 'grp'), may hold values from -2 to 2, as said below
- gain: bfloat16 [8192], P('grp'), may hold values from 0.099609375 to 1.8984375
- lengths: int32 [32], replicated, may hold values from 1 to 1024, 8192 in all
Outputs:
- normed: bfloat16 [8192, 8192], P('ctx', 'grp')
Inputs may be any that keep to these rules, and one draw needn't show every extreme that they name: The lengths sum to 8192, and one document has exactly 1024 tokens. `query`: gate values of order one. `filt`: filter taps of order one or less.
All inputs are finite; a program needn't handle non-finite values.
Results may differ from a plain program's by a relative error of at most 0.0049.
Values may be sent and summed in bfloat16 or wider, within the bound.
A program may use at most 64 MiB of HBM per device.

v0:
```python
from functools import partial

import jax
import jax.numpy as jnp
from jax import lax
from jax.sharding import PartitionSpec as P

DOC_BLOCKS = 8


def passed_along(value, axis, steps):
    count = lax.axis_size(axis)
    leading, last = (max(0, -steps), min(count, count - steps))
    return lax.ppermute(value, axis, [(source, source + steps) for source in range(leading, last)])


def doc_numbers(lengths, first, entry_total):
    ends = jnp.cumsum(lengths)
    where = first + lax.iota(jnp.int32, entry_total)
    return jnp.sum((ends[None, :] <= where[:, None]).astype(jnp.int32), axis=1)


def band_rows(filt_rows, shift, rows):
    index = lax.iota(jnp.int32, rows)
    kernel_offset = shift * rows + index[:, None] - index[None, :]
    inside = (kernel_offset >= 0) & (kernel_offset < filt_rows.shape[1])
    picked = jnp.take(filt_rows, jnp.clip(kernel_offset, 0, filt_rows.shape[1] - 1), axis=1)
    return jnp.where(inside[None, :, :], picked, jnp.zeros_like(picked))


def apply_rows(kern, source):
    width, rows = source.shape
    groups = kern.shape[0]
    grouped = source.reshape(groups, width // groups, rows)
    out = jnp.einsum("gts,gcs->gct", kern, grouped, preferred_element_type=jnp.float32)
    return out.reshape(width, rows)


def far_term(filt_rows, shift, source, cols, rowm):
    kern = band_rows(filt_rows, shift, source.shape[1])
    masked = jnp.where(cols[None, :], source, jnp.zeros_like(source))
    return apply_rows(kern, masked) * rowm[None, :].astype(jnp.float32)


def zero_term(source, cols, rowm):
    return jnp.zeros(source.shape, jnp.float32)


def shards(query, key_in, value, filt, gain, lengths):
    rows, width = query.shape
    signal = (key_in.astype(jnp.float32) * value.astype(jnp.float32)).astype(jnp.bfloat16)
    full_filter = lax.all_gather(filt, "ctx", axis=0, tiled=True)
    filt_rows = full_filter.T
    start = lax.axis_index("ctx") * rows
    signal_rows = signal.T
    mine = doc_numbers(lengths, start, rows)
    same = mine[:, None] == mine[None, :]
    diag_kern = band_rows(filt_rows, 0, rows)
    diag_kern = jnp.where(same[None, :, :], diag_kern, jnp.zeros_like(diag_kern))
    conv_rows = apply_rows(diag_kern, signal_rows)
    first = mine[0]
    rowm = mine == first
    for shift in range(1, DOC_BLOCKS + 1):
        source = passed_along(signal_rows, "ctx", shift)
        begin = start - shift * rows
        preceding_tokens = doc_numbers(lengths, begin, rows)
        cols = (preceding_tokens == first) & (begin >= 0)
        conv_rows = conv_rows + lax.cond(
            jnp.any(cols), partial(far_term, filt_rows, shift), zero_term, source, cols, rowm
        )
    conv = conv_rows.T
    gated = query.astype(jnp.float32) * conv
    power = lax.psum(jnp.sum(gated * gated, axis=1), "grp")
    scale = lax.rsqrt(power / (width * lax.axis_size("grp")) + 1e-05)
    return (gated * scale[:, None] * gain.astype(jnp.float32)[None, :]).astype(jnp.bfloat16)


def solution(mesh):
    placed = (P("ctx", "grp"), P("ctx", "grp"), P("ctx", "grp"), P("ctx", "grp"), P("grp"), P())
    return jax.shard_map(
        shards, mesh=mesh, in_specs=placed, out_specs=P("ctx", "grp"), check_vma=False
    )
```

profile of v0, /device:TPU:197, one launch (start us, length us, event | category | flops | bytes accessed | tf_op | source)
XLA Modules:
  0.0 703.2 jit_solution(4480050742871907952)
XLA Ops:
  6.4 5.1 collective-permute-start.1
  14.1 4.4 collective-permute-start.3
  23.7 50.4 %all_gather.3 = bf16[1024,64]{1,0:T(8,128)(2,1)S(1)} all-gather(bf16[16,64]{1,0:T(8,128)(2,1)S(1)} %copy-done.3), channel_id=1, replica_groups=mesh['ctx'=64,'grp'=8] {'ctx'}, dimensions={0}, use_global_device_ids=true | all-gather | bytes 133120 | tf_op jit(solution)/shard_map/all_gather | solution.py:52
  74.1 57.4 %gather_fusion.8 = bf16[16384,64]{1,0:T(8,128)(2,1)} fusion(bf16[64,1024]{0,1:T(8,128)(2,1)S(1)} %bitcast.100, s32[16384]{0:T(1024)S(1)} %bitcast_clamp_fusion.8), kind=kCustom, calls=%fused_computation.8.clone | custom fusion | bytes 4259840 | tf_op jit(solution)/shard_map/jit(_take)/gather | solution.py:27
  131.5 4.8 copy.60
  143.4 5.2 collective-permute-start.5
  150.9 4.3 collective-permute-start.7
  161.2 64.9 %conditional.8 = (f32[1024,128]{0,1:T(8,128)S(1)}) conditional(s32[]{:T(128)} %convert_element_type.107, () %tuple.54, (pred[128]{0:T(512)(128)(4,1)S(1)}, bf16[1024,128]{1,0:T(8,128)(2,1)}, bf16[64,1024]{0,1:T(8,128)(2,1)S(1)}, pred[128]{0:T(512)(128)(4,1)S(1)}) %tuple.132), branch_computations={%region_4.6_spmd, %region_5.7_spmd} | conditional | flops 36192512 | bytes 14093064 | solution.py:68
  161.5 57.4 %gather_fusion = bf16[16384,64]{1,0:T(8,128)(2,1)} fusion(bf16[64,1024]{0,1:T(8,128)(2,1)S(1)} %get-tuple-element.89, s32[16384]{0:T(1024)S(1)} %bitcast_clamp_fusion), kind=kCustom, calls=%fused_computation.clone | custom fusion | bytes 4259840 | tf_op jit(solution)/shard_map/cond/branch_1_fun/jit(_take)/gather | solution.py:27
  218.8 4.8 copy.49
  226.1 65.7 %conditional.9 = (f32[1024,128]{0,1:T(8,128)}) conditional(s32[]{:T(128)} %convert_element_type.109, () %tuple.56, (pred[128]{0:T(512)(128)(4,1)S(1)}, bf16[1024,128]{1,0:T(8,128)(2,1)}, bf16[64,1024]{0,1:T(8,128)(2,1)S(1)}, pred[128]{0:T(512)(128)(4,1)S(1)}) %tuple.141), branch_computations={%region_8.10_spmd, %region_9.11_spmd} | conditional | flops 36192512 | bytes 14093064 | solution.py:68
  226.4 57.4 %gather_fusion.1 = bf16[16384,64]{1,0:T(8,128)(2,1)} fusion(bf16[64,1024]{0,1:T(8,128)(2,1)S(1)} %get-tuple-element.98, s32[16384]{0:T(1024)S(1)} %bitcast_clamp_fusion.1), kind=kCustom, calls=%fused_computation.1.clone | custom fusion | bytes 4259840 | tf_op jit(solution)/shard_map/cond/branch_1_fun/jit(_take)/gather | solution.py:27
  283.8 4.8 copy.50
  291.8 65.7 %conditional.10 = (f32[1024,128]{0,1:T(8,128)}) conditional(s32[]{:T(128)} %convert_element_type.111, () %tuple.58, (pred[128]{0:T(512)(128)(4,1)S(1)}, bf16[1024,128]{1,0:T(8,128)(2,1)}, bf16[64,1024]{0,1:T(8,128)(2,1)S(1)}, pred[128]{0:T(512)(128)(4,1)S(1)}) %tuple.140), branch_computations={%region_12.14_spmd, %region_13.15_spmd} | conditional | flops 36192512 | bytes 14093064 | solution.py:68
  292.1 57.4 %gather_fusion.2 = bf16[16384,64]{1,0:T(8,128)(2,1)} fusion(bf16[64,1024]{0,1:T(8,128)(2,1)S(1)} %get-tuple-element.104, s32[16384]{0:T(1024)S(1)} %bitcast_clamp_fusion.2), kind=kCustom, calls=%fused_computation.2.clone | custom fusion | bytes 4259840 | tf_op jit(solution)/shard_map/cond/branch_1_fun/jit(_take)/gather | solution.py:27
  349.4 4.8 copy.51
  357.5 65.7 %conditional.11 = (f32[1024,128]{0,1:T(8,128)}) conditional(s32[]{:T(128)} %convert_element_type.113, () %tuple.60, (pred[128]{0:T(512)(128)(4,1)S(1)}, bf16[1024,128]{1,0:T(8,128)(2,1)}, bf16[64,1024]{0,1:T(8,128)(2,1)S(1)}, pred[128]{0:T(512)(128)(4,1)S(1)}) %tuple.135), branch_computations={%region_16.18_spmd, %region_17.19_spmd} | conditional | flops 36192512 | bytes 14093064 | solution.py:68
  357.8 57.4 %gather_fusion.3 = bf16[16384,64]{1,0:T(8,128)(2,1)} fusion(bf16[64,1024]{0,1:T(8,128)(2,1)S(1)} %get-tuple-element.108, s32[16384]{0:T(1024)S(1)} %bitcast_clamp_fusion.3), kind=kCustom, calls=%fused_computation.3.clone | custom fusion | bytes 4259840 | tf_op jit(solution)/shard_map/cond/branch_1_fun/jit(_take)/gather | solution.py:27
  415.1 4.8 copy.52
  423.2 65.7 %conditional.12 = (f32[1024,128]{0,1:T(8,128)}) conditional(s32[]{:T(128)} %convert_element_type.115, () %tuple.62, (pred[128]{0:T(512)(128)(4,1)S(1)}, bf16[1024,128]{1,0:T(8,128)(2,1)}, bf16[64,1024]{0,1:T(8,128)(2,1)S(1)}, pred[128]{0:T(512)(128)(4,1)S(1)}) %tuple.136), branch_computations={%region_20.22_spmd, %region_21.23_spmd} | conditional | flops 36192512 | bytes 14093064 | solution.py:68
  423.5 57.4 %gather_fusion.4 = bf16[16384,64]{1,0:T(8,128)(2,1)} fusion(bf16[64,1024]{0,1:T(8,128)(2,1)S(1)} %get-tuple-element.112, s32[16384]{0:T(1024)S(1)} %bitcast_clamp_fusion.4), kind=kCustom, calls=%fused_computation.4.clone | custom fusion | bytes 4259840 | tf_op jit(solution)/shard_map/cond/branch_1_fun/jit(_take)/gather | solution.py:27
  480.8 4.8 copy.53
  488.9 65.7 %conditional.13 = (f32[1024,128]{0,1:T(8,128)}) conditional(s32[]{:T(128)} %convert_element_type.117, () %tuple.64, (pred[128]{0:T(512)(128)(4,1)S(1)}, bf16[1024,128]{1,0:T(8,128)(2,1)}, bf16[64,1024]{0,1:T(8,128)(2,1)S(1)}, pred[128]{0:T(512)(128)(4,1)S(1)}) %tuple.137), branch_computations={%region_24.26_spmd, %region_25.27_spmd} | conditional | flops 36192512 | bytes 14093064 | solution.py:68
  489.2 57.4 %gather_fusion.5 = bf16[16384,64]{1,0:T(8,128)(2,1)} fusion(bf16[64,1024]{0,1:T(8,128)(2,1)S(1)} %get-tuple-element.116, s32[16384]{0:T(1024)S(1)} %bitcast_clamp_fusion.5), kind=kCustom, calls=%fused_computation.5.clone | custom fusion | bytes 4259840 | tf_op jit(solution)/shard_map/cond/branch_1_fun/jit(_take)/gather | solution.py:27
  546.5 4.8 copy.54
  554.6 65.7 %conditional.14 = (f32[1024,128]{0,1:T(8,128)}) conditional(s32[]{:T(128)} %convert_element_type.119, () %tuple.66, (pred[128]{0:T(512)(128)(4,1)S(1)}, bf16[1024,128]{1,0:T(8,128)(2,1)}, bf16[64,1024]{0,1:T(8,128)(2,1)S(1)}, pred[128]{0:T(512)(128)(4,1)S(1)}) %tuple.138), branch_computations={%region_28.30_spmd, %region_29.31_spmd} | conditional | flops 36192512 | bytes 14093064 | solution.py:68
  554.8 57.4 %gather_fusion.6 = bf16[16384,64]{1,0:T(8,128)(2,1)} fusion(bf16[64,1024]{0,1:T(8,128)(2,1)S(1)} %get-tuple-element.120, s32[16384]{0:T(1024)S(1)} %bitcast_clamp_fusion.6), kind=kCustom, calls=%fused_computation.6.clone | custom fusion | bytes 4259840 | tf_op jit(solution)/shard_map/cond/branch_1_fun/jit(_take)/gather | solution.py:27
  612.2 4.8 copy.55
  620.3 65.7 %conditional.15 = (f32[1024,128]{0,1:T(8,128)}) conditional(s32[]{:T(128)} %convert_element_type.121, () %tuple.68, (pred[128]{0:T(512)(128)(4,1)S(1)}, bf16[1024,128]{1,0:T(8,128)(2,1)}, bf16[64,1024]{0,1:T(8,128)(2,1)S(1)}, pred[128]{0:T(512)(128)(4,1)S(1)}) %tuple.139), branch_computations={%region_32.34_spmd, %region_33.35_spmd} | conditional | flops 36192512 | bytes 14093064 | solution.py:68
  620.6 57.4 %gather_fusion.7 = bf16[16384,64]{1,0:T(8,128)(2,1)} fusion(bf16[64,1024]{0,1:T(8,128)(2,1)S(1)} %get-tuple-element.124, s32[16384]{0:T(1024)S(1)} %bitcast_clamp_fusion.7), kind=kCustom, calls=%fused_computation.7.clone | custom fusion | bytes 4259840 | tf_op jit(solution)/shard_map/cond/branch_1_fun/jit(_take)/gather | solution.py:27
  678.0 4.8 copy.56
  688.5 13.9 %psum.7 = f32[128]{0:T(128)S(1)} all-reduce(f32[128]{0:T(128)S(1)} %get-tuple-element.143), channel_id=1, replica_groups=mesh['ctx'=64,'grp'=8] {'grp'}, use_global_device_ids=true, to_apply=%region_35.37 | all-reduce | flops 128 | bytes 1024 | tf_op jit(solution)/shard_map/psum | solution.py:73
  (116 shorter events, 54.4 us)
Async XLA Ops:
  0.0 23.7 %copy-start.3 = (bf16[16,64]{1,0:T(8,128)(2,1)S(1)}, bf16[16,64]{1,0:T(8,128)(2,1)}, u32[]{:S(2)}) copy-start(bf16[16,64]{1,0:T(8,128)(2,1)} %param.27) | copy-start | bytes 6148
  3.0 140.3 %collective-permute-start = (bf16[1024,128]{1,0:T(8,128)(2,1)}, bf16[1024,128]{1,0:T(8,128)(2,1)}, u32[]{:S(2)}, u32[]{:S(2)}) collective-permute-start(bf16[1024,128]{1,0:T(8,128)(2,1)} %bitcast.40), channel_id=1, source_target_pairs={{0,8},{8,16},{16,24},{24,32},{32,40},{40,48},{48,56},{56,64},{64,7... | collective-permute-start | bytes 786440 | tf_op jit(solution)/shard_map/ppermute | solution.py:14
  6.4 142.2 %collective-permute-start.1 = (bf16[1024,128]{1,0:T(8,128)(2,1)}, bf16[1024,128]{1,0:T(8,128)(2,1)S(1)}, u32[]{:S(2)}, u32[]{:S(2)}) collective-permute-start(bf16[1024,128]{1,0:T(8,128)(2,1)} %bitcast.40), channel_id=1, source_target_pairs={{0,16},{8,24},{16,32},{24,40},{32,48},{40,56},{48,64},{56,72},{64,... | collective-permute-start | bytes 786440 | tf_op jit(solution)/shard_map/ppermute | solution.py:14
  11.6 139.3 %collective-permute-start.2 = (bf16[1024,128]{1,0:T(8,128)(2,1)}, bf16[1024,128]{1,0:T(8,128)(2,1)S(1)}, u32[]{:S(2)}, u32[]{:S(2)}) collective-permute-start(bf16[1024,128]{1,0:T(8,128)(2,1)} %bitcast.40), channel_id=1, source_target_pairs={{0,24},{8,32},{16,40},{24,48},{32,56},{40,64},{48,72},{56,80},{64,... | collective-permute-start | bytes 786440 | tf_op jit(solution)/shard_map/ppermute | solution.py:14
  14.1 343.4 %collective-permute-start.3 = (bf16[1024,128]{1,0:T(8,128)(2,1)}, bf16[1024,128]{1,0:T(8,128)(2,1)}, u32[]{:S(2)}, u32[]{:S(2)}) collective-permute-start(bf16[1024,128]{1,0:T(8,128)(2,1)} %bitcast.40), channel_id=1, source_target_pairs={{0,32},{8,40},{16,48},{24,56},{32,64},{40,72},{48,80},{56,88},{64,... | collective-permute-start | bytes 786440 | tf_op jit(solution)/shard_map/ppermute | solution.py:14
  18.5 404.8 %collective-permute-start.4 = (bf16[1024,128]{1,0:T(8,128)(2,1)}, bf16[1024,128]{1,0:T(8,128)(2,1)}, u32[]{:S(2)}, u32[]{:S(2)}) collective-permute-start(bf16[1024,128]{1,0:T(8,128)(2,1)} %bitcast.40), channel_id=1, source_target_pairs={{0,40},{8,48},{16,56},{24,64},{32,72},{40,80},{48,88},{56,96},{64,... | collective-permute-start | bytes 786440 | tf_op jit(solution)/shard_map/ppermute | solution.py:14
  139.8 21.3 %copy-start.4 = (bf16[1024]{0:T(1024)(128)(2,1)S(1)}, bf16[1024]{0:T(1024)(128)(2,1)}, u32[]{:S(2)}) copy-start(bf16[1024]{0:T(1024)(128)(2,1)} %param.28) | copy-start | bytes 6148
  143.4 345.5 %collective-permute-start.5 = (bf16[1024,128]{1,0:T(8,128)(2,1)}, bf16[1024,128]{1,0:T(8,128)(2,1)}, u32[]{:S(2)}, u32[]{:S(2)}) collective-permute-start(bf16[1024,128]{1,0:T(8,128)(2,1)} %bitcast.40), channel_id=1, source_target_pairs={{0,48},{8,56},{16,64},{24,72},{32,80},{40,88},{48,96},{56,104},{64... | collective-permute-start | bytes 786440 | tf_op jit(solution)/shard_map/ppermute | solution.py:14
  148.6 7.3 %copy-start.2 = (bf16[1024,128]{1,0:T(8,128)(2,1)}, bf16[1024,128]{1,0:T(8,128)(2,1)S(1)}, u32[]{:S(2)}) copy-start(bf16[1024,128]{1,0:T(8,128)(2,1)S(1)} %collective-permute-done.1) | copy-start | bytes 786436
  148.7 406.0 %collective-permute-start.6 = (bf16[1024,128]{1,0:T(8,128)(2,1)}, bf16[1024,128]{1,0:T(8,128)(2,1)}, u32[]{:S(2)}, u32[]{:S(2)}) collective-permute-start(bf16[1024,128]{1,0:T(8,128)(2,1)} %bitcast.40), channel_id=1, source_target_pairs={{0,56},{8,64},{16,72},{24,80},{32,88},{40,96},{48,104},{56,112},{6... | collective-permute-start | bytes 786440 | tf_op jit(solution)/shard_map/ppermute | solution.py:14
  150.9 5.0 copy-start.1
  150.9 469.4 %collective-permute-start.7 = (bf16[1024,128]{1,0:T(8,128)(2,1)}, bf16[1024,128]{1,0:T(8,128)(2,1)}, u32[]{:S(2)}, u32[]{:S(2)}) collective-permute-start(bf16[1024,128]{1,0:T(8,128)(2,1)} %bitcast.40), channel_id=1, source_target_pairs={{0,64},{8,72},{16,80},{24,88},{32,96},{40,104},{48,112},{56,120},{... | collective-permute-start | bytes 786440 | tf_op jit(solution)/shard_map/ppermute | solution.py:14
  620.3 65.7 %copy-start = (bf16[128,1024]{1,0:T(8,128)(2,1)S(1)}, bf16[128,1024]{1,0:T(8,128)(2,1)}, u32[]{:S(2)}) copy-start(bf16[128,1024]{1,0:T(8,128)(2,1)} %param.24) | copy-start | bytes 786436
where the time goes:
time: 706 us; the launch traced here: 703 us
  local copies, waits for them, and re-layouts  570 us (81%)
  blocking collectives  64.3 us (9%)
  starting transfers between devices  31.1 us (4%)
  other arithmetic  20.3 us (3%)
  matrix products  11.6 us (2%)
    gather x18, local copies, waits for them, and re-layouts, band_rows(): jnp.take(filt_rows, jnp.clip(kernel_offset, 0, filt_rows.shape[1] - 1), a...  560 us
    all_gather x1, blocking collectives, shards(): full_filter = lax.all_gather(filt, 'ctx', axis=0, tiled=True)  50.4 us
    ppermute x8, starting transfers between devices, passed_along(): lax.ppermute(value, axis, [(source, source + steps) for source in range(l...  31.1 us
  transfers between devices with their start and end apart: 8, of which 0 were waited for; matrix products, arithmetic and copies ran while one was open for 75% of the time, Pallas kernels for 0%

commit v1 on v0

--- a/solution.py
+++ b/solution.py
@@ -15,7 +15,8 @@
 
 
 def doc_numbers(lengths, first, entry_total):
-    ends = jnp.cumsum(lengths)
+    number = lax.iota(jnp.int32, lengths.shape[0])
+    ends = jnp.sum(jnp.where(number[None, :] <= number[:, None], lengths[None, :], 0), axis=1)
     where = first + lax.iota(jnp.int32, entry_total)
     return jnp.sum((ends[None, :] <= where[:, None]).astype(jnp.int32), axis=1)
 

time: 706 us -> 696 us (0.986)
  the two profiles are of different devices: /device:TPU:197 before, /device:TPU:455 now
where the time goes in v1:
time: 696 us; the launch traced here: 694 us
  local copies, waits for them, and re-layouts  570 us (82%)
  blocking collectives  76.3 us (11%)
  other arithmetic  21 us (3%)
  matrix products  11.6 us (2%)
  starting transfers between devices  10.3 us (1%)
    gather x18, local copies, waits for them, and re-layouts, band_rows(): jnp.take(filt_rows, jnp.clip(kernel_offset, 0, filt_rows.shape[1] - 1), a...  560 us
    all_gather x1, blocking collectives, shards(): full_filter = lax.all_gather(filt, 'ctx', axis=0, tiled=True)  62.5 us
  transfers between devices with their start and end apart: 8, of which 0 were waited for; matrix products, arithmetic and copies ran while one was open for 76% of the time, Pallas kernels for 0%

profile of v1, /device:TPU:455, one launch (start us, length us, event | category | flops | bytes accessed | tf_op | source)
XLA Modules:
  0.0 694.4 jit_solution(9272428493507254910)
XLA Ops:
  4.3 1.3 collective-permute-start.1
  5.6 1.3 collective-permute-start.2
  10.7 62.5 %all_gather.3 = bf16[1024,64]{1,0:T(8,128)(2,1)S(1)} all-gather(bf16[16,64]{1,0:T(8,128)(2,1)} %param.27), channel_id=1, replica_groups=mesh['ctx'=64,'grp'=8] {'ctx'}, dimensions={0}, use_global_device_ids=true | all-gather | bytes 133120 | tf_op jit(solution)/shard_map/all_gather | solution.py:53
  73.1 57.4 %gather_fusion.8 = bf16[16384,64]{1,0:T(8,128)(2,1)} fusion(bf16[64,1024]{0,1:T(8,128)(2,1)S(1)} %bitcast.99, s32[16384]{0:T(1024)S(1)} %bitcast_clamp_fusion.8), kind=kCustom, calls=%fused_computation.8.clone | custom fusion | bytes 4259840 | tf_op jit(solution)/shard_map/jit(_take)/gather | solution.py:28
  130.5 4.8 copy.37
  138.8 2.1 fusion.113
  152.3 64.9 %conditional.8 = (f32[1024,128]{0,1:T(8,128)S(1)}) conditional(s32[]{:T(128)} %convert_element_type.107, () %tuple.54, (pred[128]{0:T(512)(128)(4,1)S(1)}, bf16[1024,128]{1,0:T(8,128)(2,1)}, bf16[64,1024]{0,1:T(8,128)(2,1)S(1)}, pred[128]{0:T(512)(128)(4,1)S(1)}) %tuple.132), branch_computations={%region_4.6_spmd, %region_5.7_spmd} | conditional | flops 36192512 | bytes 14093064 | solution.py:69
  152.6 57.4 %gather_fusion = bf16[16384,64]{1,0:T(8,128)(2,1)} fusion(bf16[64,1024]{0,1:T(8,128)(2,1)S(1)} %get-tuple-element.89, s32[16384]{0:T(1024)S(1)} %bitcast_clamp_fusion), kind=kCustom, calls=%fused_computation.clone | custom fusion | bytes 4259840 | tf_op jit(solution)/shard_map/cond/branch_1_fun/jit(_take)/gather | solution.py:28
  210.0 4.8 copy.27
  217.3 65.7 %conditional.9 = (f32[1024,128]{0,1:T(8,128)}) conditional(s32[]{:T(128)} %convert_element_type.109, () %tuple.56, (pred[128]{0:T(512)(128)(4,1)S(1)}, bf16[1024,128]{1,0:T(8,128)(2,1)}, bf16[64,1024]{0,1:T(8,128)(2,1)S(1)}, pred[128]{0:T(512)(128)(4,1)S(1)}) %tuple.141), branch_computations={%region_8.10_spmd, %region_9.11_spmd} | conditional | flops 36192512 | bytes 14093064 | solution.py:69
  217.5 57.4 %gather_fusion.1 = bf16[16384,64]{1,0:T(8,128)(2,1)} fusion(bf16[64,1024]{0,1:T(8,128)(2,1)S(1)} %get-tuple-element.98, s32[16384]{0:T(1024)S(1)} %bitcast_clamp_fusion.1), kind=kCustom, calls=%fused_computation.1.clone | custom fusion | bytes 4259840 | tf_op jit(solution)/shard_map/cond/branch_1_fun/jit(_take)/gather | solution.py:28
  274.9 4.8 copy.28
  283.0 65.7 %conditional.10 = (f32[1024,128]{0,1:T(8,128)}) conditional(s32[]{:T(128)} %convert_element_type.111, () %tuple.58, (pred[128]{0:T(512)(128)(4,1)S(1)}, bf16[1024,128]{1,0:T(8,128)(2,1)}, bf16[64,1024]{0,1:T(8,128)(2,1)S(1)}, pred[128]{0:T(512)(128)(4,1)S(1)}) %tuple.140), branch_computations={%region_12.14_spmd, %region_13.15_spmd} | conditional | flops 36192512 | bytes 14093064 | solution.py:69
  283.2 57.4 %gather_fusion.2 = bf16[16384,64]{1,0:T(8,128)(2,1)} fusion(bf16[64,1024]{0,1:T(8,128)(2,1)S(1)} %get-tuple-element.104, s32[16384]{0:T(1024)S(1)} %bitcast_clamp_fusion.2), kind=kCustom, calls=%fused_computation.2.clone | custom fusion | bytes 4259840 | tf_op jit(solution)/shard_map/cond/branch_1_fun/jit(_take)/gather | solution.py:28
  340.6 4.8 copy.29
  348.7 65.7 %conditional.11 = (f32[1024,128]{0,1:T(8,128)}) conditional(s32[]{:T(128)} %convert_element_type.113, () %tuple.60, (pred[128]{0:T(512)(128)(4,1)S(1)}, bf16[1024,128]{1,0:T(8,128)(2,1)}, bf16[64,1024]{0,1:T(8,128)(2,1)S(1)}, pred[128]{0:T(512)(128)(4,1)S(1)}) %tuple.135), branch_computations={%region_16.18_spmd, %region_17.19_spmd} | conditional | flops 36192512 | bytes 14093064 | solution.py:69
  348.9 57.4 %gather_fusion.3 = bf16[16384,64]{1,0:T(8,128)(2,1)} fusion(bf16[64,1024]{0,1:T(8,128)(2,1)S(1)} %get-tuple-element.108, s32[16384]{0:T(1024)S(1)} %bitcast_clamp_fusion.3), kind=kCustom, calls=%fused_computation.3.clone | custom fusion | bytes 4259840 | tf_op jit(solution)/shard_map/cond/branch_1_fun/jit(_take)/gather | solution.py:28
  406.3 4.8 copy.30
  414.4 65.7 %conditional.12 = (f32[1024,128]{0,1:T(8,128)}) conditional(s32[]{:T(128)} %convert_element_type.115, () %tuple.62, (pred[128]{0:T(512)(128)(4,1)S(1)}, bf16[1024,128]{1,0:T(8,128)(2,1)}, bf16[64,1024]{0,1:T(8,128)(2,1)S(1)}, pred[128]{0:T(512)(128)(4,1)S(1)}) %tuple.136), branch_computations={%region_20.22_spmd, %region_21.23_spmd} | conditional | flops 36192512 | bytes 14093064 | solution.py:69
  414.6 57.4 %gather_fusion.4 = bf16[16384,64]{1,0:T(8,128)(2,1)} fusion(bf16[64,1024]{0,1:T(8,128)(2,1)S(1)} %get-tuple-element.112, s32[16384]{0:T(1024)S(1)} %bitcast_clamp_fusion.4), kind=kCustom, calls=%fused_computation.4.clone | custom fusion | bytes 4259840 | tf_op jit(solution)/shard_map/cond/branch_1_fun/jit(_take)/gather | solution.py:28
  472.0 4.8 copy.31
  480.1 65.7 %conditional.13 = (f32[1024,128]{0,1:T(8,128)}) conditional(s32[]{:T(128)} %convert_element_type.117, () %tuple.64, (pred[128]{0:T(512)(128)(4,1)S(1)}, bf16[1024,128]{1,0:T(8,128)(2,1)}, bf16[64,1024]{0,1:T(8,128)(2,1)S(1)}, pred[128]{0:T(512)(128)(4,1)S(1)}) %tuple.137), branch_computations={%region_24.26_spmd, %region_25.27_spmd} | conditional | flops 36192512 | bytes 14093064 | solution.py:69
  480.3 57.4 %gather_fusion.5 = bf16[16384,64]{1,0:T(8,128)(2,1)} fusion(bf16[64,1024]{0,1:T(8,128)(2,1)S(1)} %get-tuple-element.116, s32[16384]{0:T(1024)S(1)} %bitcast_clamp_fusion.5), kind=kCustom, calls=%fused_computation.5.clone | custom fusion | bytes 4259840 | tf_op jit(solution)/shard_map/cond/branch_1_fun/jit(_take)/gather | solution.py:28
  537.7 4.8 copy.32
  545.8 65.7 %conditional.14 = (f32[1024,128]{0,1:T(8,128)}) conditional(s32[]{:T(128)} %convert_element_type.119, () %tuple.66, (pred[128]{0:T(512)(128)(4,1)S(1)}, bf16[1024,128]{1,0:T(8,128)(2,1)}, bf16[64,1024]{0,1:T(8,128)(2,1)S(1)}, pred[128]{0:T(512)(128)(4,1)S(1)}) %tuple.138), branch_computations={%region_28.30_spmd, %region_29.31_spmd} | conditional | flops 36192512 | bytes 14093064 | solution.py:69
  546.0 57.4 %gather_fusion.6 = bf16[16384,64]{1,0:T(8,128)(2,1)} fusion(bf16[64,1024]{0,1:T(8,128)(2,1)S(1)} %get-tuple-element.120, s32[16384]{0:T(1024)S(1)} %bitcast_clamp_fusion.6), kind=kCustom, calls=%fused_computation.6.clone | custom fusion | bytes 4259840 | tf_op jit(solution)/shard_map/cond/branch_1_fun/jit(_take)/gather | solution.py:28
  603.4 4.8 copy.33
  611.5 65.7 %conditional.15 = (f32[1024,128]{0,1:T(8,128)}) conditional(s32[]{:T(128)} %convert_element_type.121, () %tuple.68, (pred[128]{0:T(512)(128)(4,1)S(1)}, bf16[1024,128]{1,0:T(8,128)(2,1)}, bf16[64,1024]{0,1:T(8,128)(2,1)S(1)}, pred[128]{0:T(512)(128)(4,1)S(1)}) %tuple.139), branch_computations={%region_32.34_spmd, %region_33.35_spmd} | conditional | flops 36192512 | bytes 14093064 | solution.py:69
  611.7 57.4 %gather_fusion.7 = bf16[16384,64]{1,0:T(8,128)(2,1)} fusion(bf16[64,1024]{0,1:T(8,128)(2,1)S(1)} %get-tuple-element.124, s32[16384]{0:T(1024)S(1)} %bitcast_clamp_fusion.7), kind=kCustom, calls=%fused_computation.7.clone | custom fusion | bytes 4259840 | tf_op jit(solution)/shard_map/cond/branch_1_fun/jit(_take)/gather | solution.py:28
  669.1 4.8 copy.34
  677.2 2.6 multiply_reduce_fusion
  679.7 13.9 %psum.7 = f32[128]{0:T(128)S(1)} all-reduce(f32[128]{0:T(128)S(1)} %get-tuple-element.143), channel_id=1, replica_groups=mesh['ctx'=64,'grp'=8] {'grp'}, use_global_device_ids=true, to_apply=%region_35.37 | all-reduce | flops 128 | bytes 1024 | tf_op jit(solution)/shard_map/psum | solution.py:74
  (110 shorter events, 45.3 us)
Async XLA Ops:
  3.0 139.4 %collective-permute-start = (bf16[1024,128]{1,0:T(8,128)(2,1)}, bf16[1024,128]{1,0:T(8,128)(2,1)}, u32[]{:S(2)}, u32[]{:S(2)}) collective-permute-start(bf16[1024,128]{1,0:T(8,128)(2,1)} %bitcast.40), channel_id=1, source_target_pairs={{0,8},{8,16},{16,24},{24,32},{32,40},{40,48},{48,56},{56,64},{64,7... | collective-permute-start | bytes 786440 | tf_op jit(solution)/shard_map/ppermute | solution.py:14
  4.3 139.4 %collective-permute-start.1 = (bf16[1024,128]{1,0:T(8,128)(2,1)}, bf16[1024,128]{1,0:T(8,128)(2,1)S(1)}, u32[]{:S(2)}, u32[]{:S(2)}) collective-permute-start(bf16[1024,128]{1,0:T(8,128)(2,1)} %bitcast.40), channel_id=1, source_target_pairs={{0,16},{8,24},{16,32},{24,40},{32,48},{40,56},{48,64},{56,72},{64,... | collective-permute-start | bytes 786440 | tf_op jit(solution)/shard_map/ppermute | solution.py:14
  5.6 139.4 %collective-permute-start.2 = (bf16[1024,128]{1,0:T(8,128)(2,1)}, bf16[1024,128]{1,0:T(8,128)(2,1)S(1)}, u32[]{:S(2)}, u32[]{:S(2)}) collective-permute-start(bf16[1024,128]{1,0:T(8,128)(2,1)} %bitcast.40), channel_id=1, source_target_pairs={{0,24},{8,32},{16,40},{24,48},{32,56},{40,64},{48,72},{56,80},{64,... | collective-permute-start | bytes 786440 | tf_op jit(solution)/shard_map/ppermute | solution.py:14
  6.9 341.8 %collective-permute-start.3 = (bf16[1024,128]{1,0:T(8,128)(2,1)}, bf16[1024,128]{1,0:T(8,128)(2,1)}, u32[]{:S(2)}, u32[]{:S(2)}) collective-permute-start(bf16[1024,128]{1,0:T(8,128)(2,1)} %bitcast.40), channel_id=1, source_target_pairs={{0,32},{8,40},{16,48},{24,56},{32,64},{40,72},{48,80},{56,88},{64,... | collective-permute-start | bytes 786440 | tf_op jit(solution)/shard_map/ppermute | solution.py:14
  8.2 406.1 %collective-permute-start.4 = (bf16[1024,128]{1,0:T(8,128)(2,1)}, bf16[1024,128]{1,0:T(8,128)(2,1)}, u32[]{:S(2)}, u32[]{:S(2)}) collective-permute-start(bf16[1024,128]{1,0:T(8,128)(2,1)} %bitcast.40), channel_id=1, source_target_pairs={{0,40},{8,48},{16,56},{24,64},{32,72},{40,80},{48,88},{56,96},{64,... | collective-permute-start | bytes 786440 | tf_op jit(solution)/shard_map/ppermute | solution.py:14
  138.8 13.4 %copy-start.2 = (bf16[1024]{0:T(1024)(128)(2,1)S(1)}, bf16[1024]{0:T(1024)(128)(2,1)}, u32[]{:S(2)}) copy-start(bf16[1024]{0:T(1024)(128)(2,1)} %param.28) | copy-start | bytes 6148
  142.4 337.6 %collective-permute-start.5 = (bf16[1024,128]{1,0:T(8,128)(2,1)}, bf16[1024,128]{1,0:T(8,128)(2,1)}, u32[]{:S(2)}, u32[]{:S(2)}) collective-permute-start(bf16[1024,128]{1,0:T(8,128)(2,1)} %bitcast.40), channel_id=1, source_target_pairs={{0,48},{8,56},{16,64},{24,72},{32,80},{40,88},{48,96},{56,104},{64... | collective-permute-start | bytes 786440 | tf_op jit(solution)/shard_map/ppermute | solution.py:14
  143.7 3.3 copy-start.1
  143.7 402.0 %collective-permute-start.6 = (bf16[1024,128]{1,0:T(8,128)(2,1)}, bf16[1024,128]{1,0:T(8,128)(2,1)}, u32[]{:S(2)}, u32[]{:S(2)}) collective-permute-start(bf16[1024,128]{1,0:T(8,128)(2,1)} %bitcast.40), channel_id=1, source_target_pairs={{0,56},{8,64},{16,72},{24,80},{32,88},{40,96},{48,104},{56,112},{6... | collective-permute-start | bytes 786440 | tf_op jit(solution)/shard_map/ppermute | solution.py:14
  145.0 2.0 copy-start
  145.1 466.4 %collective-permute-start.7 = (bf16[1024,128]{1,0:T(8,128)(2,1)}, bf16[1024,128]{1,0:T(8,128)(2,1)}, u32[]{:S(2)}, u32[]{:S(2)}) collective-permute-start(bf16[1024,128]{1,0:T(8,128)(2,1)} %bitcast.40), channel_id=1, source_target_pairs={{0,64},{8,72},{16,80},{24,88},{32,96},{40,104},{48,112},{56,120},{... | collective-permute-start | bytes 786440 | tf_op jit(solution)/shard_map/ppermute | solution.py:14

commit v2 on v0

v2 whole, which is shorter than its diff:
```python
from functools import partial

import jax
import jax.numpy as jnp
from jax import lax
from jax.experimental import pallas as pl
from jax.experimental.pallas import tpu as pltpu
from jax.sharding import PartitionSpec as P

LONGEST = 1024
EPS = 1e-05
MESH = pl.DeviceIdType.MESH
BF16, F32 = jnp.bfloat16, jnp.float32


def kernel(
    sizes, lengths_hbm, filt_hbm, gain_hbm, query, key_in, value, out,
    lengths, filt, gain, q, k_buf, v_buf, fpad, fsend, frecv, ff, xsend, xin, wfar, w0, srcmask, diagmask, xm,
    outbuf, cin, gated, pw, load_sem,
    f1_s, f1_r, f2_s, f2_r, x_s, x_r, h_s, h_r, o_s, o_r, p_s, p_r,
):
    per, planes, across, rows, width, taps, docs = sizes
    groups = filt.shape[1]
    mine, per_group = groups // per, width // groups
    wide = width // per
    me, y = lax.axis_index("ctx"), lax.axis_index("grp")
    z, j = me // per, me % per

    def at(plane, place):
        return (lax.rem(plane, planes) * per + lax.rem(place, per), y)

    loads = [
        pltpu.make_async_copy(src, dst, load_sem.at[i])
        for i, (src, dst) in enumerate((
            (key_in, k_buf), (value, v_buf), (query, q), (filt_hbm, filt), (lengths_hbm, lengths), (gain_hbm, gain)
        ))
    ]
    for load in loads:
        load.start()

    barrier = pltpu.get_barrier_semaphore()
    before = [at(z, j + d) for d in range(1, per)]
    before += [at(z + planes - 1, j + d) for d in range(per)]
    before += [at(z + d, j) for d in range(1, planes - 1)]
    before += [(me, lax.rem(y + d, across)) for d in range(1, across)]
    for device in before:
        pl.semaphore_signal(barrier, inc=1, device_id=device, device_id_type=MESH)

    fpad[...] = jnp.zeros_like(fpad)
    loads[3].wait()
    fpad[pl.ds(pl.multiple_of(j * taps, taps), taps), 0:groups] = filt[...].astype(F32)
    by_group = jnp.transpose(fpad[...])
    for d in range(per):
        fsend[d] = by_group[d * mine:(d + 1) * mine]

    loads[0].wait()
    loads[1].wait()
    for d in range(per):
        cols = slice(d * wide, (d + 1) * wide)
        signal = k_buf[:, cols].astype(F32) * v_buf[:, cols].astype(F32)
        xsend[d] = jnp.transpose(signal).astype(BF16)

    pl.semaphore_wait(barrier, len(before))

    def send(src, dst, send_sem, recv_sem, device):
        copy = pltpu.make_async_remote_copy(
            src_ref=src, dst_ref=dst, send_sem=send_sem, recv_sem=recv_sem, device_id=device, device_id_type=MESH
        )
        copy.start()
        return copy

    f1, halo, plane = [], [], []
    for d in range(1, per):
        to = lax.rem(j + d, per)
        f1.append(send(fsend.at[to], frecv.at[j], f1_s.at[d], f1_r.at[d], at(z, j + d)))
    for d in range(per):
        to = lax.rem(j + d, per)
        halo.append(send(xsend.at[to], xin.at[j], h_s.at[d], h_r.at[d], at(z + 1, j + d)))
        if d:
            plane.append(send(xsend.at[to], xin.at[per + j], x_s.at[d], x_r.at[d], at(z, j + d)))
    xin[per + j] = xsend[j]
    frecv[j] = fsend[j]

    loads[4].wait()
    base = z * (per * rows)
    block = lax.broadcasted_iota(jnp.int32, (per, rows), 0)
    lane = lax.broadcasted_iota(jnp.int32, (per, rows), 1)
    head = base + block * rows
    token = head + lane
    end, start, first = jnp.int32(0), jnp.zeros_like(token), jnp.zeros_like(token)
    for m in range(docs):
        end = end + lengths[m]
        start = jnp.where(end <= token, end, start)
        first = jnp.where(end <= head, end, first)
    reach = (start < head).astype(F32)
    for lag in range(1, per + 1):
        keep = (token - lag * rows >= first).astype(F32)
        for a in range(per):
            srcmask[a * per + lag - 1] = jnp.broadcast_to(keep[a:a + 1], (per_group, rows)).astype(BF16)
    source = lax.broadcasted_iota(jnp.int32, (rows, rows), 0)
    target = lax.broadcasted_iota(jnp.int32, (rows, rows), 1)
    within = start - head
    for a in range(per):
        diagmask[a] = (source >= within[a:a + 1]).astype(F32).astype(BF16)

    for copy in f1:
        copy.wait_recv()
    taps_here = frecv[0]
    for d in range(1, per):
        taps_here = taps_here + frecv[d]
    ff[z] = taps_here
    f2 = [
        send(ff.at[z], ff.at[z], f2_s.at[d], f2_r.at[d], at(z + d, j)) for d in range(1, planes)
    ]
    for copy in f2:
        copy.wait_recv()

    causal = target >= source

    def build(g, carry):
        last = None
        for lag in range(min(per, planes)):
            row = jnp.broadcast_to(ff[lag, pl.ds(g, 1), :], (rows, rows))
            turned = pltpu.roll(row, 0, 1, stride=1, stride_axis=0)
            if lag == 0:
                w0[g] = jnp.where(causal, turned, 0.0).astype(BF16)
            else:
                wfar[g, (lag - 1) * rows:lag * rows, :] = jnp.where(causal, turned, last).astype(BF16)
            last = turned
        for lag in range(min(per, planes), per + 1):
            ended = jnp.where(causal, 0.0, last) if lag == planes else jnp.zeros_like(last)
            wfar[g, (lag - 1) * rows:lag * rows, :] = ended.astype(BF16)
        return carry

    lax.fori_loop(0, mine, build, 0)

    for copy in plane + halo:
        copy.wait_recv()

    def convolve(g, carry):
        part = pl.ds(pl.multiple_of(g * per_group, per_group), per_group)
        for a in range(per):
            for lag in range(1, per + 1):
                xm[a * per_group:(a + 1) * per_group, (lag - 1) * rows:lag * rows] = (
                    xin[per + a - lag, part, :] * srcmask[a * per + lag - 1]
                )
        far = jnp.dot(xm[...], wfar[g], preferred_element_type=F32)
        near = w0[g]
        for a in range(per):
            own = jnp.dot(xin[per + a, part, :], near * diagmask[a], preferred_element_type=F32)
            conv = far[a * per_group:(a + 1) * per_group] * reach[a:a + 1] + own
            outbuf[a, part, :] = conv.astype(BF16)
        return carry

    lax.fori_loop(0, mine, convolve, 0)

    back = []
    for d in range(1, per):
        to = lax.rem(j + d, per)
        back.append(send(outbuf.at[to], cin.at[j], o_s.at[d], o_r.at[d], at(z, j + d)))
    cin[j] = outbuf[j]
    loads[2].wait()
    total = jnp.zeros((rows, wide), F32)
    for d in range(per):
        if d:
            back[d - 1].wait_recv()
        origin = lax.rem(j + per - d, per)
        cols = pl.ds(pl.multiple_of(origin * wide, wide), wide)
        conv = jnp.transpose(cin[origin].astype(F32))
        some = q[:, cols].astype(F32) * conv
        gated[:, cols] = some
        total = total + some * some
    power = jnp.sum(jnp.transpose(total), axis=0, keepdims=True)
    pw[y] = jnp.broadcast_to(power, pw.shape[1:])
    shared = [
        send(pw.at[y], pw.at[y], p_s.at[d], p_r.at[d], (me, lax.rem(y + d, across))) for d in range(1, across)
    ]
    for copy in shared:
        copy.wait_recv()
    power = pw[0]
    for d in range(1, across):
        power = power + pw[d]
    scale = lax.rsqrt(power / (width * across) + EPS)
    scale = jnp.transpose(jnp.broadcast_to(scale[0:1], (rows, rows)))
    loads[5].wait()
    for d in range(per):
        cols = slice(d * wide, (d + 1) * wide)
        weight = gain[cols].astype(F32).reshape(1, wide)
        out[:, cols] = (gated[:, cols] * scale * weight).astype(BF16)
    for copy in f1 + halo + plane + f2 + back + shared:
        copy.wait_send()


def shards(query, key_in, value, filt, gain, lengths):
    rows, width = query.shape
    taps, groups = filt.shape
    per = LONGEST // rows
    planes, across = lax.axis_size("ctx") // per, lax.axis_size("grp")
    mine, wide = groups // per, width // per
    sizes = (per, planes, across, rows, width, taps, lengths.shape[0])
    vmem, dma = pltpu.VMEM, pltpu.SemaphoreType.DMA
    return pl.pallas_call(
        partial(kernel, sizes),
        out_shape=jax.ShapeDtypeStruct((rows, width), BF16),
        in_specs=[pl.BlockSpec(memory_space=pltpu.HBM)] * 6,
        out_specs=pl.BlockSpec(memory_space=vmem),
        scratch_shapes=[
            pltpu.SMEM(lengths.shape, jnp.int32),
            vmem(filt.shape, BF16),
            vmem(gain.shape, BF16),
            vmem((rows, width), BF16),
            vmem((rows, width), BF16),
            vmem((rows, width), BF16),
            vmem((rows, rows), F32),
            vmem((per, mine, rows), F32),
            vmem((per, mine, rows), F32),
            vmem((planes, mine, rows), F32),
            vmem((per, wide, rows), BF16),
            vmem((2 * per, wide, rows), BF16),
            vmem((mine, per * rows, rows), BF16),
            vmem((mine, rows, rows), BF16),
            vmem((per * per, width // groups, rows), BF16),
            vmem((per, rows, rows), BF16),
            vmem((per * (width // groups), per * rows), BF16),
            vmem((per, wide, rows), BF16),
            vmem((per, wide, rows), BF16),
            vmem((rows, width), F32),
            vmem((across, 8, rows), F32),
            dma((6,)),
            dma((per,)), dma((per,)),
            dma((planes,)), dma((planes,)),
            dma((per,)), dma((per,)),
            dma((per,)), dma((per,)),
            dma((per,)), dma((per,)),
            dma((across,)), dma((across,)),
        ],
        compiler_params=pltpu.CompilerParams(
            collective_id=0, has_side_effects=True, vmem_limit_bytes=65000 * 1024
        ),
    )(lengths, filt, gain, query, key_in, value)


def solution(mesh):
    placed = (P("ctx", "grp"), P("ctx", "grp"), P("ctx", "grp"), P("ctx", "grp"), P("grp"), P())
    return jax.shard_map(
        shards, mesh=mesh, in_specs=placed, out_specs=P("ctx", "grp"), check_vma=False
    )
```

time: 706 us -> 40.7 us (0.06)
  the two profiles are of different devices: /device:TPU:197 before, /device:TPU:1 now
where the time goes in v2:
time: 40.7 us; the launch traced here: 40.5 us
  Pallas kernels  38.9 us (96%)
  local copies, waits for them, and re-layouts  1.67 us (4%)
    pallas_call x1, Pallas kernels, shards(): pl.pallas_call(partial(kernel, sizes), out_shape=jax.ShapeDtypeStruct((ro...  38.9 us
    unnamed x1, local copies, waits for them, and re-layouts  1.67 us

profile of v2, /device:TPU:1, one launch (start us, length us, event | category | flops | bytes accessed | tf_op | source)
XLA Modules:
  0.0 40.5 jit_solution(7815945986495582880)
XLA Ops:
  0.0 38.9 %shard_map.64 = bf16[128,1024]{1,0:T(8,128)(2,1)} custom-call(s32[32]{0:T(128)} %lengths_hbm.1, bf16[16,64]{1,0:T(8,128)(2,1)} %filt_hbm.1, bf16[1024]{0:T(1024)(128)(2,1)} %gain_hbm.1, bf16[128,1024]{1,0:T(8,128)(2,1)} %query.1, bf16[128,1024]{1,0:T(8,128)(2,1)} %key_in.1, bf16[128,1024]{1,0:T(8,128)(2,1)} %value.1), custom_call_target="tpu_custom_call" | custom-call | tf_op jit(solution)/shard_map/pallas_call | solution.py:202
  38.9 1.7 %copy.8 = bf16[128,1024]{1,0:T(8,128)(2,1)} copy(bf16[128,1024]{1,0:T(8,128)(2,1)} %shard_map.64) | data formatting | bytes 524288

commit v3 on v2

v3 whole, which is shorter than its diff:
```python
from functools import partial

import jax
import jax.numpy as jnp
from jax import lax
from jax.experimental import pallas as pl
from jax.experimental.pallas import tpu as pltpu
from jax.sharding import PartitionSpec as P

LONGEST = 1024
EARLY = 3
EPS = 1e-05
MESH = pl.DeviceIdType.MESH
BF16, F32 = jnp.bfloat16, jnp.float32


def kernel(
    sizes, lengths_hbm, filt_hbm, gain_hbm, query, key_in, value, out,
    lengths, filt, gain, q, k_buf, v_buf, fpad, fsend, frecv, ff, turned, xsend, xin, wfar, w0, diagmask, xm,
    acc, outbuf, cin, gated, pw, load_sem,
    f1_s, f1_r, f2_s, f2_r, x_s, x_r, h_s, h_r, o_s, o_r, p_s, p_r, hello,
):
    per, planes, across, rows, width, taps, docs = sizes
    groups = filt.shape[1]
    mine, per_group = groups // per, width // groups
    wide = width // per
    me, y = lax.axis_index("ctx"), lax.axis_index("grp")
    z, j = me // per, me % per
    chip, core = j // 2, j % 2
    chips = per // 2

    def place(dx, dc):
        return lax.rem(chip + dx, chips) * 2 + lax.rem(core + dc, 2)

    def in_plane(to):
        return (z * per + to, y)

    def in_column(d):
        return (lax.rem(z + d, planes) * per + j, y)

    order = list(dict.fromkeys([0] + [dx for pair in zip(range(1, chips), range(chips - 1, 0, -1)) for dx in pair]))
    peers = [(dx, dc, dx * 2 + dc) for dx in order for dc in (0, 1)][1:]

    loads = [
        pltpu.make_async_copy(src, dst, load_sem.at[i])
        for i, (src, dst) in enumerate((
            (filt_hbm, filt), (key_in, k_buf), (value, v_buf), (lengths_hbm, lengths), (query, q), (gain_hbm, gain)
        ))
    ]
    for load in loads:
        load.start()

    barrier = pltpu.get_barrier_semaphore()

    def greet(device):
        pl.semaphore_signal(barrier, inc=1, device_id=device, device_id_type=MESH)

    for dx, dc, _ in peers:
        greet(in_plane(place(dx, dc)))
    for d in range(1, across):
        greet((me, lax.rem(y + d, across)))
    greet(in_column(planes - 1))
    for d in range(1, planes - 1):
        pl.when(z + d < planes)(partial(greet, in_column(d)))
    greeted = (per - 1) + (across - 1) + z + jnp.where(z < planes - 1, 1, 0)

    fpad[...] = jnp.zeros_like(fpad)
    loads[0].wait()
    fpad[pl.ds(pl.multiple_of(j * taps, taps), taps), 0:groups] = filt[...].astype(F32)
    by_group = jnp.transpose(fpad[...])
    for d in range(per):
        fsend[d] = by_group[d * mine:(d + 1) * mine]

    loads[1].wait()
    loads[2].wait()
    for b in range(per):
        cols = slice(b * wide, (b + 1) * wide)
        signal = k_buf[:, cols].astype(F32) * v_buf[:, cols].astype(F32)
        xsend[b] = jnp.transpose(signal).astype(BF16)

    pl.semaphore_wait(barrier, greeted)

    def copy_to(src, dst, send_sem, recv_sem, device):
        return pltpu.make_async_remote_copy(
            src_ref=src, dst_ref=dst, send_sem=send_sem, recv_sem=recv_sem, device_id=device, device_id_type=MESH
        )

    def send(*what):
        copy = copy_to(*what)
        copy.start()
        return copy

    for d in range(1, planes):
        @pl.when(z >= d)
        def _():
            pl.semaphore_signal(hello.at[d], inc=1, device_id=in_column(planes - d), device_id_type=MESH)

    f1, plane = [], []
    for dx, dc, n in peers:
        to = place(dx, dc)
        f1.append(send(fsend.at[to], frecv.at[j], f1_s.at[n], f1_r.at[n], in_plane(to)))
    for dx, dc, n in peers:
        to = place(dx, dc)
        plane.append(send(xsend.at[to], xin.at[per + j], x_s.at[n], x_r.at[n], in_plane(to)))
    halo = [copy_to(xsend.at[j], xin.at[j], h_s.at[0], h_r.at[0], in_column(1))]
    for dx, dc, n in peers:
        origin = place(chips - dx, 2 - dc)
        halo.append(copy_to(xin.at[per + origin], xin.at[origin], h_s.at[n], h_r.at[n], in_column(1)))
    pl.when(z < planes - 1)(halo[0].start)
    xin[per + j] = xsend[j]
    frecv[j] = fsend[j]

    @pl.when(z == 0)
    def _():
        xin[0:per] = jnp.zeros((per, wide, rows), BF16)

    loads[3].wait()
    base = z * (per * rows)
    block = lax.broadcasted_iota(jnp.int32, (per, rows), 0)
    lane = lax.broadcasted_iota(jnp.int32, (per, rows), 1)
    ahead = base + block * rows
    token = ahead + lane
    end, start, first = jnp.int32(0), jnp.zeros_like(token), jnp.zeros_like(token)
    for m in range(docs):
        end = end + lengths[m]
        start = jnp.where(end <= token, end, start)
        first = jnp.where(end <= ahead, end, first)

    for copy in f1:
        copy.wait_recv()
    taps_here = frecv[0]
    for d in range(1, per):
        taps_here = taps_here + frecv[d]
    ff[z] = taps_here
    f2 = [copy_to(ff.at[z], ff.at[z], f2_s.at[d], f2_r.at[d], in_column(d)) for d in range(1, planes)]
    for d in range(1, planes):
        pl.when(z + d >= planes)(f2[d - 1].start)

    for copy, following in zip(plane, halo[1:]):
        copy.wait_recv()
        pl.when(z < planes - 1)(following.start)

    reach = jnp.concatenate(
        [jnp.broadcast_to((start < ahead).astype(F32)[a:a + 1], (per_group, rows)) for a in range(per)], axis=0
    )
    source = lax.broadcasted_iota(jnp.int32, (rows, rows), 0)
    target = lax.broadcasted_iota(jnp.int32, (rows, rows), 1)
    causal = target >= source
    within = start - ahead
    for a in range(per):
        diagmask[a] = (source >= within[a:a + 1]).astype(F32).astype(BF16)

    for d in range(1, planes):
        @pl.when(z + d < planes)
        def _():
            pl.semaphore_wait(hello.at[d], 1)
            f2[d - 1].start()

    def take(other):
        @pl.when(z != other)
        def _():
            d = lax.rem(z - other + planes, planes)
            copy_to(ff.at[other], ff.at[other], f2_s.at[d], f2_r.at[d], in_column(d)).wait_recv()

    def build(lag, g, carry):
        if lag < planes:
            row = jnp.broadcast_to(ff[lag, pl.ds(g, 1), :], (rows, rows))
            now = pltpu.roll(row, 0, 1, stride=1, stride_axis=0)
        else:
            now = jnp.zeros((rows, rows), F32)
        if lag == 0:
            w0[g] = jnp.where(causal, now, 0.0).astype(BF16)
        else:
            wfar[g, (lag - 1) * rows:lag * rows, :] = jnp.where(causal, now, turned[g]).astype(BF16)
        turned[g] = now
        return carry

    def part(g):
        return pl.ds(pl.multiple_of(g * per_group, per_group), per_group)

    masks = [(token - lag * rows >= first).astype(F32) for lag in range(1, per + 1)]

    def gather(g, carry):
        for a in range(per):
            for lag in range(1, per + 1):
                keep = jnp.broadcast_to(masks[lag - 1][a:a + 1], (per_group, rows)).astype(BF16)
                xm[g, a * per_group:(a + 1) * per_group, (lag - 1) * rows:lag * rows] = (
                    xin[per + a - lag, part(g), :] * keep
                )
        return carry

    def begin(g, carry):
        far = jnp.dot(xm[g, :, 0:EARLY * rows], wfar[g, 0:EARLY * rows, :], preferred_element_type=F32) * reach
        near = w0[g]
        for a in range(per):
            own = jnp.dot(xin[per + a, part(g), :], near * diagmask[a], preferred_element_type=F32)
            here = slice(a * per_group, (a + 1) * per_group)
            acc[g, here] = far[here] + own
        return carry

    def finish(g, carry):
        far = jnp.dot(xm[g, :, EARLY * rows:], wfar[g, EARLY * rows:, :], preferred_element_type=F32)
        conv = (far * reach + acc[g]).astype(BF16)
        for a in range(per):
            outbuf[a, part(g), :] = conv[a * per_group:(a + 1) * per_group]
        return carry

    for lag in range(EARLY + 1):
        if lag < planes:
            take(lag)
        lax.fori_loop(0, mine, partial(build, lag), 0, unroll=True)
    for copy in halo:
        pl.when(z > 0)(copy.wait_recv)
    lax.fori_loop(0, mine, gather, 0, unroll=True)
    lax.fori_loop(0, mine, begin, 0, unroll=True)
    for lag in range(EARLY + 1, per + 1):
        if lag < planes:
            take(lag)
        lax.fori_loop(0, mine, partial(build, lag), 0, unroll=True)
    lax.fori_loop(0, mine, finish, 0, unroll=True)

    back = []
    for dx, dc, n in peers:
        to = place(dx, dc)
        back.append(send(outbuf.at[to], cin.at[j], o_s.at[n], o_r.at[n], in_plane(to)))
    cin[j] = outbuf[j]
    loads[4].wait()
    total = jnp.zeros((rows, wide), F32)
    for copy, (dx, dc, n) in zip([None] + back, [(0, 0, 0)] + peers):
        if copy is not None:
            copy.wait_recv()
        origin = place(chips - dx, 2 - dc)
        cols = pl.ds(pl.multiple_of(origin * wide, wide), wide)
        conv = jnp.transpose(cin[origin].astype(F32))
        some = q[:, cols].astype(F32) * conv
        gated[:, cols] = some
        total = total + some * some
    power = jnp.sum(jnp.transpose(total), axis=0, keepdims=True)
    pw[y] = jnp.broadcast_to(power, pw.shape[1:])
    shared = [
        send(pw.at[y], pw.at[y], p_s.at[d], p_r.at[d], (me, lax.rem(y + d, across))) for d in range(1, across)
    ]
    for copy in shared:
        copy.wait_recv()
    power = pw[0]
    for d in range(1, across):
        power = power + pw[d]
    scale = lax.rsqrt(power / (width * across) + EPS)
    scale = jnp.transpose(jnp.broadcast_to(scale[0:1], (rows, rows)))
    loads[5].wait()
    for d in range(per):
        cols = slice(d * wide, (d + 1) * wide)
        weight = gain[cols].astype(F32).reshape(1, wide)
        out[:, cols] = (gated[:, cols] * scale * weight).astype(BF16)
    for copy in f1 + f2 + plane + back + shared:
        copy.wait_send()
    for copy in halo:
        pl.when(z < planes - 1)(copy.wait_send)


def shards(query, key_in, value, filt, gain, lengths):
    rows, width = query.shape
    taps, groups = filt.shape
    per = LONGEST // rows
    planes, across = lax.axis_size("ctx") // per, lax.axis_size("grp")
    mine, wide = groups // per, width // per
    sizes = (per, planes, across, rows, width, taps, lengths.shape[0])
    vmem, dma = pltpu.VMEM, pltpu.SemaphoreType.DMA
    return pl.pallas_call(
        partial(kernel, sizes),
        out_shape=jax.ShapeDtypeStruct((rows, width), BF16),
        in_specs=[pl.BlockSpec(memory_space=pltpu.HBM)] * 6,
        out_specs=pl.BlockSpec(memory_space=vmem),
        scratch_shapes=[
            pltpu.SMEM(lengths.shape, jnp.int32),
            vmem(filt.shape, BF16),
            vmem(gain.shape, BF16),
            vmem((rows, width), BF16),
            vmem((rows, width), BF16),
            vmem((rows, width), BF16),
            vmem((rows, rows), F32),
            vmem((per, mine, rows), F32),
            vmem((per, mine, rows), F32),
            vmem((planes, mine, rows), F32),
            vmem((mine, rows, rows), F32),
            vmem((per, wide, rows), BF16),
            vmem((2 * per, wide, rows), BF16),
            vmem((mine, per * rows, rows), BF16),
            vmem((mine, rows, rows), BF16),
            vmem((per, rows, rows), BF16),
            vmem((mine, per * (width // groups), per * rows), BF16),
            vmem((mine, per * (width // groups), rows), F32),
            vmem((per, wide, rows), BF16),
            vmem((per, wide, rows), BF16),
            vmem((rows, width), F32),
            vmem((across, 8, rows), F32),
            dma((6,)),
            dma((per,)), dma((per,)),
            dma((planes,)), dma((planes,)),
            dma((per,)), dma((per,)),
            dma((per,)), dma((per,)),
            dma((per,)), dma((per,)),
            dma((across,)), dma((across,)),
            pltpu.SemaphoreType.REGULAR((planes,)),
        ],
        compiler_params=pltpu.CompilerParams(
            collective_id=0, has_side_effects=True, vmem_limit_bytes=65000 * 1024
        ),
    )(lengths, filt, gain, query, key_in, value)


def solution(mesh):
    placed = (P("ctx", "grp"), P("ctx", "grp"), P("ctx", "grp"), P("ctx", "grp"), P("grp"), P())
    return jax.shard_map(
        shards, mesh=mesh, in_specs=placed, out_specs=P("ctx", "grp"), check_vma=False
    )
```

time: 40.7 us -> 35.4 us (0.87)
  Pallas kernels: 38.9 us -> 33.6 us
    pallas_call x1, Pallas kernels: 38.9 us -> 33.6 us  [shards(): pl.pallas_call(partial(kernel, sizes), out_shape=jax.ShapeDtypeStruct((ro...]
where the time goes in v3:
time: 35.4 us; the launch traced here: 35.2 us
  Pallas kernels  33.6 us (95%)
  local copies, waits for them, and re-layouts  1.67 us (5%)
    pallas_call x1, Pallas kernels, shards(): pl.pallas_call(partial(kernel, sizes), out_shape=jax.ShapeDtypeStruct((ro...  33.6 us
    unnamed x1, local copies, waits for them, and re-layouts  1.67 us

profile of v3, /device:TPU:1, one launch (start us, length us, event | category | flops | bytes accessed | tf_op | source)
XLA Modules:
  0.0 35.2 jit_solution(17976118072409012501)
XLA Ops:
  0.0 33.6 %shard_map.64 = bf16[128,1024]{1,0:T(8,128)(2,1)} custom-call(s32[32]{0:T(128)} %lengths_hbm.1, bf16[16,64]{1,0:T(8,128)(2,1)} %filt_hbm.1, bf16[1024]{0:T(1024)(128)(2,1)} %gain_hbm.1, bf16[128,1024]{1,0:T(8,128)(2,1)} %query.1, bf16[128,1024]{1,0:T(8,128)(2,1)} %key_in.1, bf16[128,1024]{1,0:T(8,128)(2,1)} %value.1), custom_call_target="tpu_custom_call" | custom-call | tf_op jit(solution)/shard_map/pallas_call | solution.py:269
  33.6 1.7 %copy.8 = bf16[128,1024]{1,0:T(8,128)(2,1)} copy(bf16[128,1024]{1,0:T(8,128)(2,1)} %shard_map.64) | data formatting | bytes 524288

commit v4 on v3

--- a/solution.py
+++ b/solution.py
@@ -16,9 +16,9 @@
 
 def kernel(
     sizes, lengths_hbm, filt_hbm, gain_hbm, query, key_in, value, out,
-    lengths, filt, gain, q, k_buf, v_buf, fpad, fsend, frecv, ff, turned, xsend, xin, wfar, w0, diagmask, xm,
-    acc, outbuf, cin, gated, pw, load_sem,
-    f1_s, f1_r, f2_s, f2_r, x_s, x_r, h_s, h_r, o_s, o_r, p_s, p_r, hello,
+    lengths, filt, gain, q_buf, k_buf, v_buf, fpad, fsend, frecv, ff, turned, xsend, xin, qsend, qin, wfar, w0, diagmask, xm,
+    acc, outbuf, cin, gated, pw, psend, precv, load_sem,
+    f1_s, f1_r, f2_s, f2_r, x_s, x_r, q_s, q_r, h_s, h_r, o_s, o_r, p_s, p_r, t_s, t_r, hello,
 ):
     per, planes, across, rows, width, taps, docs = sizes
     groups = filt.shape[1]
@@ -44,7 +44,7 @@
     loads = [
         pltpu.make_async_copy(src, dst, load_sem.at[i])
         for i, (src, dst) in enumerate((
-            (filt_hbm, filt), (key_in, k_buf), (value, v_buf), (lengths_hbm, lengths), (query, q), (gain_hbm, gain)
+            (filt_hbm, filt), (key_in, k_buf), (value, v_buf), (lengths_hbm, lengths), (query, q_buf), (gain_hbm, gain)
         ))
     ]
     for load in loads:
@@ -139,6 +139,16 @@
     for copy, following in zip(plane, halo[1:]):
         copy.wait_recv()
         pl.when(z < planes - 1)(following.start)
+
+    loads[4].wait()
+    asked = []
+    for b in range(per):
+        cols = slice(b * wide, (b + 1) * wide)
+        qsend[b] = jnp.transpose(q_buf[:, cols].astype(F32)).astype(BF16)
+    for dx, dc, n in peers:
+        to = place(dx, dc)
+        asked.append(send(qsend.at[to], qin.at[j], q_s.at[n], q_r.at[n], in_plane(to)))
+    qin[j] = qsend[j]
 
     reach = jnp.concatenate(
         [jnp.broadcast_to((start < ahead).astype(F32)[a:a + 1], (per_group, rows)) for a in range(per)], axis=0
@@ -200,10 +210,13 @@
 
     def finish(g, carry):
         far = jnp.dot(xm[g, :, EARLY * rows:], wfar[g, EARLY * rows:, :], preferred_element_type=F32)
-        conv = (far * reach + acc[g]).astype(BF16)
+        conv = far * reach + acc[g]
+        sums = []
         for a in range(per):
-            outbuf[a, part(g), :] = conv[a * per_group:(a + 1) * per_group]
-        return carry
+            some = conv[a * per_group:(a + 1) * per_group] * qin[a, part(g), :].astype(F32)
+            outbuf[a, part(g), :] = some.astype(BF16)
+            sums.append(jnp.sum((some * some).reshape(per_group // 8, 8, rows), axis=0))
+        return carry + jnp.stack(sums)
 
     for lag in range(EARLY + 1):
         if lag < planes:
@@ -217,34 +230,40 @@
         if lag < planes:
             take(lag)
         lax.fori_loop(0, mine, partial(build, lag), 0, unroll=True)
-    lax.fori_loop(0, mine, finish, 0, unroll=True)
-
+    for copy in asked:
+        copy.wait_recv()
+    power = lax.fori_loop(0, mine, finish, jnp.zeros((per, 8, rows), F32), unroll=True)
+
+    pw[y] = jnp.sum(power, axis=1)
+    shared = [
+        send(pw.at[y], pw.at[y], p_s.at[d], p_r.at[d], (me, lax.rem(y + d, across))) for d in range(1, across)
+    ]
     back = []
     for dx, dc, n in peers:
         to = place(dx, dc)
         back.append(send(outbuf.at[to], cin.at[j], o_s.at[n], o_r.at[n], in_plane(to)))
     cin[j] = outbuf[j]
-    loads[4].wait()
-    total = jnp.zeros((rows, wide), F32)
+    for copy in shared:
+        copy.wait_recv()
+    power = pw[0]
+    for d in range(1, across):
+        power = power + pw[d]
+    for a in range(per):
+        psend[a] = jnp.broadcast_to(power[a:a + 1], (8, rows))
+    totals = []
+    for dx, dc, n in peers:
+        to = place(dx, dc)
+        totals.append(send(psend.at[to, 0:1], precv.at[j, 0:1], t_s.at[n], t_r.at[n], in_plane(to)))
+    precv[j] = psend[j]
     for copy, (dx, dc, n) in zip([None] + back, [(0, 0, 0)] + peers):
         if copy is not None:
             copy.wait_recv()
         origin = place(chips - dx, 2 - dc)
         cols = pl.ds(pl.multiple_of(origin * wide, wide), wide)
-        conv = jnp.transpose(cin[origin].astype(F32))
-        some = q[:, cols].astype(F32) * conv
-        gated[:, cols] = some
-        total = total + some * some
-    power = jnp.sum(jnp.transpose(total), axis=0, keepdims=True)
-    pw[y] = jnp.broadcast_to(power, pw.shape[1:])
-    shared = [
-        send(pw.at[y], pw.at[y], p_s.at[d], p_r.at[d], (me, lax.rem(y + d, across))) for d in range(1, across)
-    ]
-    for copy in shared:
-        copy.wait_recv()
-    power = pw[0]
-    for d in range(1, across):
-        power = power + pw[d]
+        gated[:, cols] = jnp.transpose(cin[origin].astype(F32))
+    for copy in totals:
+        copy.wait_recv()
+    power = jnp.sum(precv[:, 0:1], axis=0)
     scale = lax.rsqrt(power / (width * across) + EPS)
     scale = jnp.transpose(jnp.broadcast_to(scale[0:1], (rows, rows)))
     loads[5].wait()
@@ -252,7 +271,7 @@
         cols = slice(d * wide, (d + 1) * wide)
         weight = gain[cols].astype(F32).reshape(1, wide)
         out[:, cols] = (gated[:, cols] * scale * weight).astype(BF16)
-    for copy in f1 + f2 + plane + back + shared:
+    for copy in f1 + f2 + plane + asked + back + shared + totals:
         copy.wait_send()
     for copy in halo:
         pl.when(z < planes - 1)(copy.wait_send)
@@ -285,6 +304,8 @@
             vmem((mine, rows, rows), F32),
             vmem((per, wide, rows), BF16),
             vmem((2 * per, wide, rows), BF16),
+            vmem((per, wide, rows), BF16),
+            vmem((per, wide, rows), BF16),
             vmem((mine, per * rows, rows), BF16),
             vmem((mine, rows, rows), BF16),
             vmem((per, rows, rows), BF16),
@@ -293,20 +314,24 @@
             vmem((per, wide, rows), BF16),
             vmem((per, wide, rows), BF16),
             vmem((rows, width), F32),
-            vmem((across, 8, rows), F32),
+            vmem((across, per, rows), F32),
+            vmem((per, 8, rows), F32),
+            vmem((per, 8, rows), F32),
             dma((6,)),
             dma((per,)), dma((per,)),
             dma((planes,)), dma((planes,)),
             dma((per,)), dma((per,)),
             dma((per,)), dma((per,)),
             dma((per,)), dma((per,)),
+            dma((per,)), dma((per,)),
             dma((across,)), dma((across,)),
+            dma((per,)), dma((per,)),
             pltpu.SemaphoreType.REGULAR((planes,)),
         ],
         compiler_params=pltpu.CompilerParams(
-            collective_id=0, has_side_effects=True, vmem_limit_bytes=65000 * 1024
+            collective_id=0, has_side_effects=True, vmem_limit_bytes=50000 * 1024
         ),
-    )(lengths, filt, gain, query, key_in, value)
+    )(*(pltpu.with_memory_space_constraint(x, pltpu.HBM) for x in (lengths, filt, gain, query, key_in, value)))
 
 
 def solution(mesh):

time: 35.4 us -> 33.6 us (0.949)
  local copies, waits for them, and re-layouts: 1.67 us -> 0.71 us
  Pallas kernels: 33.6 us -> 32.7 us
    unnamed x1, local copies, waits for them, and re-layouts: 1.67 us -> 0.71 us
    pallas_call x1, Pallas kernels: 33.6 us -> 32.7 us  [shards(): pl.pallas_call(partial(kernel, sizes), out_shape=jax.ShapeDtypeStruct((ro...]
where the time goes in v4:
time: 33.6 us; the launch traced here: 33.4 us
  Pallas kernels  32.7 us (97%)
  local copies, waits for them, and re-layouts  0.71 us (2%)
    pallas_call x1, Pallas kernels, shards(): pl.pallas_call(partial(kernel, sizes), out_shape=jax.ShapeDtypeStruct((ro...  32.7 us
    unnamed x1, local copies, waits for them, and re-layouts  0.71 us

profile of v4, /device:TPU:1, one launch (start us, length us, event | category | flops | bytes accessed | tf_op | source)
XLA Modules:
  0.0 33.4 jit_solution(9737462910611010599)
XLA Ops:
  0.0 32.7 %shard_map.64 = bf16[128,1024]{1,0:T(8,128)(2,1)S(1)} custom-call(s32[32]{0:T(128)} %lengths_hbm.1, bf16[16,64]{1,0:T(8,128)(2,1)} %filt_hbm.1, bf16[1024]{0:T(1024)(128)(2,1)} %gain_hbm.1, bf16[128,1024]{1,0:T(8,128)(2,1)} %query.1, bf16[128,1024]{1,0:T(8,128)(2,1)} %key_in.1, bf16[128,1024]{1,0:T(8,128)(2,1)} %value.1), custom_call_target="tpu_custom_call" | custom-call | tf_op jit(solution)/shard_map/pallas_call | solution.py:288
  32.7 0.7 %copy.8 = bf16[128,1024]{1,0:T(8,128)(2,1)} copy(bf16[128,1024]{1,0:T(8,128)(2,1)S(1)} %shard_map.64) | data formatting | bytes 524288

commit v5 on v4

--- a/solution.py
+++ b/solution.py
@@ -17,8 +17,8 @@
 def kernel(
     sizes, lengths_hbm, filt_hbm, gain_hbm, query, key_in, value, out,
     lengths, filt, gain, q_buf, k_buf, v_buf, fpad, fsend, frecv, ff, turned, xsend, xin, qsend, qin, wfar, w0, diagmask, xm,
-    acc, outbuf, cin, gated, pw, psend, precv, load_sem,
-    f1_s, f1_r, f2_s, f2_r, x_s, x_r, q_s, q_r, h_s, h_r, o_s, o_r, p_s, p_r, t_s, t_r, hello,
+    acc, outbuf, cin, gated, psend, precv, load_sem,
+    f1_s, f1_r, f2_s, f2_r, x_s, x_r, q_s, q_r, h_s, h_r, o_s, o_r, p_s, p_r, hello,
 ):
     per, planes, across, rows, width, taps, docs = sizes
     groups = filt.shape[1]
@@ -234,36 +234,34 @@
         copy.wait_recv()
     power = lax.fori_loop(0, mine, finish, jnp.zeros((per, 8, rows), F32), unroll=True)
 
-    pw[y] = jnp.sum(power, axis=1)
-    shared = [
-        send(pw.at[y], pw.at[y], p_s.at[d], p_r.at[d], (me, lax.rem(y + d, across))) for d in range(1, across)
-    ]
+    power = jnp.sum(power, axis=1)
+    for a in range(per):
+        psend[a] = jnp.broadcast_to(power[a:a + 1], (8, rows))
+    mark = y * per + j
+
+    def tell(to, d):
+        other = lax.rem(y + d, across)
+        copy_to(psend.at[to, 0:1], precv.at[mark, 0:1], p_s.at[0], p_r.at[0], (z * per + to, other)).start()
+
+    for d in sorted(range(across), key=lambda d: -min(d, across - d)):
+        for dx, dc, n in [(0, 0, 0)] * (d > 0) + peers:
+            tell(place(dx, dc), d)
     back = []
     for dx, dc, n in peers:
         to = place(dx, dc)
         back.append(send(outbuf.at[to], cin.at[j], o_s.at[n], o_r.at[n], in_plane(to)))
     cin[j] = outbuf[j]
-    for copy in shared:
-        copy.wait_recv()
-    power = pw[0]
-    for d in range(1, across):
-        power = power + pw[d]
-    for a in range(per):
-        psend[a] = jnp.broadcast_to(power[a:a + 1], (8, rows))
-    totals = []
-    for dx, dc, n in peers:
-        to = place(dx, dc)
-        totals.append(send(psend.at[to, 0:1], precv.at[j, 0:1], t_s.at[n], t_r.at[n], in_plane(to)))
-    precv[j] = psend[j]
+    precv[mark] = psend[j]
     for copy, (dx, dc, n) in zip([None] + back, [(0, 0, 0)] + peers):
         if copy is not None:
             copy.wait_recv()
         origin = place(chips - dx, 2 - dc)
         cols = pl.ds(pl.multiple_of(origin * wide, wide), wide)
         gated[:, cols] = jnp.transpose(cin[origin].astype(F32))
-    for copy in totals:
-        copy.wait_recv()
-    power = jnp.sum(precv[:, 0:1], axis=0)
+    rest = precv.at[0:across * per - 1, 0:1]
+    told = copy_to(rest, rest, p_s.at[0], p_r.at[0], in_plane(place(0, 1)))
+    told.wait_recv()
+    power = jnp.sum(precv[...], axis=0)
     scale = lax.rsqrt(power / (width * across) + EPS)
     scale = jnp.transpose(jnp.broadcast_to(scale[0:1], (rows, rows)))
     loads[5].wait()
@@ -271,8 +269,9 @@
         cols = slice(d * wide, (d + 1) * wide)
         weight = gain[cols].astype(F32).reshape(1, wide)
         out[:, cols] = (gated[:, cols] * scale * weight).astype(BF16)
-    for copy in f1 + f2 + plane + asked + back + shared + totals:
+    for copy in f1 + f2 + plane + asked + back:
         copy.wait_send()
+    told.wait_send()
     for copy in halo:
         pl.when(z < planes - 1)(copy.wait_send)
 
@@ -314,9 +313,8 @@
             vmem((per, wide, rows), BF16),
             vmem((per, wide, rows), BF16),
             vmem((rows, width), F32),
-            vmem((across, per, rows), F32),
             vmem((per, 8, rows), F32),
-            vmem((per, 8, rows), F32),
+            vmem((across * per, 8, rows), F32),
             dma((6,)),
             dma((per,)), dma((per,)),
             dma((planes,)), dma((planes,)),
@@ -324,8 +322,7 @@
             dma((per,)), dma((per,)),
             dma((per,)), dma((per,)),
             dma((per,)), dma((per,)),
-            dma((across,)), dma((across,)),
-            dma((per,)), dma((per,)),
+            dma((1,)), dma((1,)),
             pltpu.SemaphoreType.REGULAR((planes,)),
         ],
         compiler_params=pltpu.CompilerParams(

time: 33.6 us -> 31.8 us (0.946)
  Pallas kernels: 32.7 us -> 30.9 us
    pallas_call x1, Pallas kernels: 32.7 us -> 30.9 us  [shards(): pl.pallas_call(partial(kernel, sizes), out_shape=jax.ShapeDtypeStruct((ro...]
where the time goes in v5:
time: 31.8 us; the launch traced here: 31.6 us
  Pallas kernels  30.9 us (97%)
  local copies, waits for them, and re-layouts  0.71 us (2%)
    pallas_call x1, Pallas kernels, shards(): pl.pallas_call(partial(kernel, sizes), out_shape=jax.ShapeDtypeStruct((ro...  30.9 us
    unnamed x1, local copies, waits for them, and re-layouts  0.71 us

profile of v5, /device:TPU:1, one launch (start us, length us, event | category | flops | bytes accessed | tf_op | source)
XLA Modules:
  0.0 31.6 jit_solution(15856561368196763927)
XLA Ops:
  0.0 30.9 %shard_map.64 = bf16[128,1024]{1,0:T(8,128)(2,1)S(1)} custom-call(s32[32]{0:T(128)} %lengths_hbm.1, bf16[16,64]{1,0:T(8,128)(2,1)} %filt_hbm.1, bf16[1024]{0:T(1024)(128)(2,1)} %gain_hbm.1, bf16[128,1024]{1,0:T(8,128)(2,1)} %query.1, bf16[128,1024]{1,0:T(8,128)(2,1)} %key_in.1, bf16[128,1024]{1,0:T(8,128)(2,1)} %value.1), custom_call_target="tpu_custom_call" | custom-call | tf_op jit(solution)/shard_map/pallas_call | solution.py:287
  30.9 0.7 %copy.8 = bf16[128,1024]{1,0:T(8,128)(2,1)} copy(bf16[128,1024]{1,0:T(8,128)(2,1)S(1)} %shard_map.64) | data formatting | bytes 524288

commit v6 on v5

--- a/solution.py
+++ b/solution.py
@@ -16,9 +16,9 @@
 
 def kernel(
     sizes, lengths_hbm, filt_hbm, gain_hbm, query, key_in, value, out,
-    lengths, filt, gain, q_buf, k_buf, v_buf, fpad, fsend, frecv, ff, turned, xsend, xin, qsend, qin, wfar, w0, diagmask, xm,
+    lengths, filt, gain, q_buf, k_buf, v_buf, fpad, fsend, frecv, fnext, ff, fl, turned, xsend, xin, qsend, qin, wfar, w0, diagmask, xm,
     acc, outbuf, cin, gated, psend, precv, load_sem,
-    f1_s, f1_r, f2_s, f2_r, x_s, x_r, q_s, q_r, h_s, h_r, o_s, o_r, p_s, p_r, hello,
+    s_s, s_r, f1_s, f1_r, f2_s, f2_r, x_s, x_r, q_s, q_r, h_s, h_r, o_s, o_r, p_s, p_r, hello,
 ):
     per, planes, across, rows, width, taps, docs = sizes
     groups = filt.shape[1]
@@ -62,14 +62,23 @@
     greet(in_column(planes - 1))
     for d in range(1, planes - 1):
         pl.when(z + d < planes)(partial(greet, in_column(d)))
-    greeted = (per - 1) + (across - 1) + z + jnp.where(z < planes - 1, 1, 0)
+    soon, late = 1, 1
+
+    @pl.when(z < soon)
+    def _():
+        for other in range(late, planes):
+            for dx, dc, _ in peers:
+                greet((other * per + place(dx, dc), y))
+
+    greeted = (per - 1) + (across - 1) + z + jnp.where(z < planes - 1, 1, 0) + jnp.where(z >= late, soon * (per - 1), 0)
 
     fpad[...] = jnp.zeros_like(fpad)
     loads[0].wait()
-    fpad[pl.ds(pl.multiple_of(j * taps, taps), taps), 0:groups] = filt[...].astype(F32)
+    fpad[0:taps, 0:groups] = filt[...].astype(F32)
     by_group = jnp.transpose(fpad[...])
     for d in range(per):
-        fsend[d] = by_group[d * mine:(d + 1) * mine]
+        spread = pltpu.roll(by_group[d * mine:(d + 1) * mine], 0, 1, stride=taps, stride_axis=0)
+        fsend[d] = jnp.broadcast_to(jnp.sum(spread, axis=0, keepdims=True), (mine, rows))
 
     loads[1].wait()
     loads[2].wait()
@@ -98,7 +107,17 @@
     f1, plane = [], []
     for dx, dc, n in peers:
         to = place(dx, dc)
-        f1.append(send(fsend.at[to], frecv.at[j], f1_s.at[n], f1_r.at[n], in_plane(to)))
+        f1.append(send(fsend.at[to, 0:1], frecv.at[j, 0:1], f1_s.at[n], f1_r.at[n], in_plane(to)))
+
+    def straight(other, to):
+        return copy_to(fsend.at[to, 0:1], fnext.at[z, j, 0:1], s_s.at[other], s_r.at[z], (other * per + to, y))
+
+    @pl.when(z >= late)
+    def _():
+        for other in range(soon):
+            for to in range(per):
+                straight(other, to).start()
+
     for dx, dc, n in peers:
         to = place(dx, dc)
         plane.append(send(xsend.at[to], xin.at[per + j], x_s.at[n], x_r.at[n], in_plane(to)))
@@ -128,13 +147,11 @@
 
     for copy in f1:
         copy.wait_recv()
-    taps_here = frecv[0]
-    for d in range(1, per):
-        taps_here = taps_here + frecv[d]
-    ff[z] = taps_here
+    ff[z] = frecv[:, 0, :]
     f2 = [copy_to(ff.at[z], ff.at[z], f2_s.at[d], f2_r.at[d], in_column(d)) for d in range(1, planes)]
     for d in range(1, planes):
-        pl.when(z + d >= planes)(f2[d - 1].start)
+        lower = z + d - planes
+        pl.when((lower >= soon) | ((lower >= 0) & (z < late)))(f2[d - 1].start)
 
     for copy, following in zip(plane, halo[1:]):
         copy.wait_recv()
@@ -166,15 +183,41 @@
             pl.semaphore_wait(hello.at[d], 1)
             f2[d - 1].start()
 
+    place_of = lax.broadcasted_iota(jnp.int32, (per, rows), 1) // taps
+    own_place = place_of == lax.broadcasted_iota(jnp.int32, (per, rows), 0)
+
+    def unpack(packed):
+        some = []
+        spread = pltpu.roll(packed, 0, 1, stride=taps, stride_axis=0)
+        for g in range(mine):
+            moved = pltpu.roll(spread, rows - g * taps, 1) if g else spread
+            some.append(jnp.sum(jnp.where(own_place, moved, 0.0), axis=0, keepdims=True))
+        return jnp.concatenate(some, axis=0)
+
     def take(other):
-        @pl.when(z != other)
-        def _():
+        def staged():
             d = lax.rem(z - other + planes, planes)
             copy_to(ff.at[other], ff.at[other], f2_s.at[d], f2_r.at[d], in_column(d)).wait_recv()
+            fl[other] = unpack(ff[other])
+
+        def direct():
+            some = fnext.at[other, :, 0:1]
+            copy_to(some, some, s_s.at[0], s_r.at[other], in_column(1)).wait_recv()
+            fl[other] = unpack(fnext[other, :, 0, :])
+
+        @pl.when(z == other)
+        def _():
+            fl[other] = unpack(ff[other])
+
+        if other >= late:
+            pl.when(z < soon)(direct)
+            pl.when((z >= soon) & (z != other))(staged)
+        else:
+            pl.when(z != other)(staged)
 
     def build(lag, g, carry):
         if lag < planes:
-            row = jnp.broadcast_to(ff[lag, pl.ds(g, 1), :], (rows, rows))
+            row = jnp.broadcast_to(fl[lag, pl.ds(g, 1), :], (rows, rows))
             now = pltpu.roll(row, 0, 1, stride=1, stride_axis=0)
         else:
             now = jnp.zeros((rows, rows), F32)
@@ -269,7 +312,17 @@
         cols = slice(d * wide, (d + 1) * wide)
         weight = gain[cols].astype(F32).reshape(1, wide)
         out[:, cols] = (gated[:, cols] * scale * weight).astype(BF16)
-    for copy in f1 + f2 + plane + asked + back:
+    for d in range(1, planes):
+        lower = z + d - planes
+        pl.when((lower < 0) | (lower >= soon) | (z < late))(f2[d - 1].wait_send)
+
+    @pl.when(z >= late)
+    def _():
+        for other in range(soon):
+            some = fsend.at[:, 0:1]
+            copy_to(some, some, s_s.at[other], s_r.at[0], in_column(1)).wait_send()
+
+    for copy in f1 + plane + asked + back:
         copy.wait_send()
     told.wait_send()
     for copy in halo:
@@ -299,6 +352,8 @@
             vmem((rows, rows), F32),
             vmem((per, mine, rows), F32),
             vmem((per, mine, rows), F32),
+            vmem((planes, per, mine, rows), F32),
+            vmem((planes, mine, rows), F32),
             vmem((planes, mine, rows), F32),
             vmem((mine, rows, rows), F32),
             vmem((per, wide, rows), BF16),
@@ -316,6 +371,7 @@
             vmem((per, 8, rows), F32),
             vmem((across * per, 8, rows), F32),
             dma((6,)),
+            dma((planes,)), dma((planes,)),
             dma((per,)), dma((per,)),
             dma((planes,)), dma((planes,)),
             dma((per,)), dma((per,)),

time: 31.8 us -> 30.4 us (0.956)
  Pallas kernels: 30.9 us -> 29.4 us
    pallas_call x1, Pallas kernels: 30.9 us -> 29.4 us  [shards(): pl.pallas_call(partial(kernel, sizes), out_shape=jax.ShapeDtypeStruct((ro...]
where the time goes in v6:
time: 30.4 us; the launch traced here: 30.2 us
  Pallas kernels  29.4 us (97%)
  local copies, waits for them, and re-layouts  0.71 us (2%)
    pallas_call x1, Pallas kernels, shards(): pl.pallas_call(partial(kernel, sizes), out_shape=jax.ShapeDtypeStruct((ro...  29.4 us
    unnamed x1, local copies, waits for them, and re-layouts  0.71 us

profile of v6, /device:TPU:1, one launch (start us, length us, event | category | flops | bytes accessed | tf_op | source)
XLA Modules:
  0.0 30.2 jit_solution(15057545721312693948)
XLA Ops:
  0.0 29.4 %shard_map.64 = bf16[128,1024]{1,0:T(8,128)(2,1)S(1)} custom-call(s32[32]{0:T(128)} %lengths_hbm.1, bf16[16,64]{1,0:T(8,128)(2,1)} %filt_hbm.1, bf16[1024]{0:T(1024)(128)(2,1)} %gain_hbm.1, bf16[128,1024]{1,0:T(8,128)(2,1)} %query.1, bf16[128,1024]{1,0:T(8,128)(2,1)} %key_in.1, bf16[128,1024]{1,0:T(8,128)(2,1)} %value.1), custom_call_target="tpu_custom_call" | custom-call | tf_op jit(solution)/shard_map/pallas_call | solution.py:340
  29.4 0.7 %copy.8 = bf16[128,1024]{1,0:T(8,128)(2,1)} copy(bf16[128,1024]{1,0:T(8,128)(2,1)S(1)} %shard_map.64) | data formatting | bytes 524288
